TPU v7x, 32 devices: a whole 2x2x4 slice. The times are simulated.
32 devices in a mesh: lon: 4 (over y, core), lat: 4 (over z), dp: 2 (over x).
Axes of the slice: x: 2, y: 2, z: 4, core: 2. Of those that a mesh axis runs over, the one named last changes fastest.
Arguments:
- tokens: bfloat16 [2, 2, 24, 48, 192], P('dp', None, 'lat', 'lon'), may hold values from -6 to 6
- grad_out: bfloat16 [2, 2, 24, 48, 192], P('dp', None, 'lat', 'lon'), may hold values from -6 to 6
- qkv_weight: bfloat16 [576, 192], P('dp'), may hold values from -0.4375 to 0.4375
- proj_weight: bfloat16 [192, 192], P('dp'), may hold values from -0.4375 to 0.4375
- norm_gain: bfloat16 [192], P('dp'), may hold values from 0.5 to 1.5
- bias_table: float32 [4, 6, 3312], P('lat'), may hold values from -2.5 to 402.5
Outputs:
- grad_tokens: bfloat16 [2, 2, 24, 48, 192], P('dp', None, 'lat', 'lon')
- grad_qkv_weight: float32 [576, 192], P('dp')
- grad_proj_weight: float32 [192, 192], P('dp')
- grad_norm_gain: float32 [192], P('dp')
- grad_bias_table: float32 [4, 6, 3312], P('lat')
All inputs are finite; a program needn't handle non-finite values.
Results may differ from a plain program's by a relative error of at most 0.015.
Values may be sent and summed in bfloat16 or wider, within the bound.
No kernel may reach another device: no remote copies, remote signals or barrier semaphores. Data moves between devices by JAX's collectives and lax.ppermute only.
A program may use at most 64 MiB of HBM per device.

v0:
```python
import math
import jax
import jax.numpy as jnp
from jax import lax
from jax.sharding import PartitionSpec as P

C = 192
H = 6
HD = 32
WZ = 2
WA = 6
WL = 12
SA = 3
SO = 6
WT = 144
POS = 3312
EPS = 1e-05
MASKED = -1e30


def passed_along(value, axis, steps):
    count = lax.axis_size(axis)
    pairs = [(source, (source + steps) % count) for source in range(count)]
    return lax.ppermute(value, axis, pairs)


def shortened(shard):
    return jax.tree.map(lambda a: a.astype(jnp.bfloat16) if a.dtype == jnp.float32 else a, shard)


def offsets_table():
    first = jnp.arange(WL)[:, None, None]
    second = jnp.arange(WL)[None, :, None]
    offset = jnp.arange(2 * WL - 1)[None, None, :]
    return (offset == first - second + WL - 1).astype(jnp.float32)


def spread_bias(table, onehot):
    window_rows = WZ * WA
    shaped = table.reshape(table.shape[0], H, window_rows, window_rows, 2 * WL - 1)
    spread = jnp.einsum("ghabr,uvr->ghaubv", shaped, onehot, precision=lax.Precision.HIGHEST)
    return spread.reshape(table.shape[0], H, WT, WT)


def gather_bias(grad_full, onehot):
    window_rows = WZ * WA
    shaped = grad_full.reshape(grad_full.shape[0], H, window_rows, WL, window_rows, WL)
    folded = jnp.einsum("ghaubv,uvr->ghabr", shaped, onehot, precision=lax.Precision.HIGHEST)
    return folded.reshape(grad_full.shape[0], H, POS)


def to_windows(grid, lat_rows, lon_cols):
    members, levels, channels = (grid.shape[0], grid.shape[1], grid.shape[4])
    lat_types = lat_rows // WA
    lon_windows = lon_cols // WL
    parts = grid.reshape(members, levels, lat_types, WA, lon_windows, WL, channels)
    parts = parts.transpose(2, 0, 4, 1, 3, 5, 6)
    return parts.reshape(lat_types, members * lon_windows, WT, channels)


def from_windows(blocks, members, lat_rows, lon_cols):
    lat_types = lat_rows // WA
    lon_windows = lon_cols // WL
    channels = blocks.shape[-1]
    parts = blocks.reshape(lat_types, members, lon_windows, WZ, WA, WL, channels)
    return parts.transpose(1, 3, 0, 4, 2, 5, 6).reshape(members, WZ, lat_rows, lon_cols, channels)


def window_grads(
    window_x, window_dy, window_flag, table, qkv_weight, proj_weight, norm_gain, onehot
):
    groups, count = (window_x.shape[0], window_x.shape[1])
    flat_x = window_x.reshape(-1, C).astype(jnp.float32)
    average = jnp.mean(flat_x, axis=-1, keepdims=True)
    centred = flat_x - average
    variance = jnp.mean(centred * centred, axis=-1, keepdims=True)
    inverse = lax.rsqrt(variance + EPS)
    unit = centred * inverse
    gain_value = norm_gain.astype(jnp.float32)
    normed = (unit * gain_value).astype(jnp.bfloat16)
    projected = jnp.dot(normed, qkv_weight.T, preferred_element_type=jnp.float32).astype(
        jnp.bfloat16
    )
    split = projected.reshape(groups, count, WT, 3, H, HD)
    queries = split[:, :, :, 0]
    key_part = split[:, :, :, 1]
    values = split[:, :, :, 2]
    head_scale = 1.0 / math.sqrt(HD)
    bias_full = spread_bias(table, onehot)
    scores = (
        jnp.einsum("gwqhd,gwkhd->gwhqk", queries, key_part, preferred_element_type=jnp.float32)
        * head_scale
    )
    scores = scores + bias_full[:, None]
    allowed = window_flag[:, :, None, :, None] == window_flag[:, :, None, None, :]
    scores = jnp.where(allowed, scores, MASKED)
    highest = jnp.max(scores, axis=-1, keepdims=True)
    expo = jnp.exp(scores - highest)
    probs = expo / jnp.sum(expo, axis=-1, keepdims=True)
    probs_low = probs.astype(jnp.bfloat16)
    attended = jnp.einsum(
        "gwhqk,gwkhd->gwqhd", probs_low, values, preferred_element_type=jnp.float32
    )
    attended = attended.astype(jnp.bfloat16).reshape(-1, C)
    flat_dy = window_dy.reshape(-1, C)
    grad_proj = jnp.dot(flat_dy.T, attended, preferred_element_type=jnp.float32)
    grad_att = jnp.dot(flat_dy, proj_weight, preferred_element_type=jnp.float32).astype(
        jnp.bfloat16
    )
    grad_att = grad_att.reshape(groups, count, WT, H, HD)
    grad_probs = jnp.einsum(
        "gwqhd,gwkhd->gwhqk", grad_att, values, preferred_element_type=jnp.float32
    )
    grad_values = jnp.einsum(
        "gwhqk,gwqhd->gwkhd", probs_low, grad_att, preferred_element_type=jnp.float32
    )
    grad_scores = probs * (grad_probs - jnp.sum(probs * grad_probs, axis=-1, keepdims=True))
    scores_low = grad_scores.astype(jnp.bfloat16)
    grad_queries = (
        jnp.einsum("gwhqk,gwkhd->gwqhd", scores_low, key_part, preferred_element_type=jnp.float32)
        * head_scale
    )
    grad_keys = (
        jnp.einsum("gwhqk,gwqhd->gwkhd", scores_low, queries, preferred_element_type=jnp.float32)
        * head_scale
    )
    grad_qkv = (
        jnp.stack([grad_queries, grad_keys, grad_values], axis=3)
        .reshape(-1, 3 * C)
        .astype(jnp.bfloat16)
    )
    grad_qkv_w = jnp.dot(grad_qkv.T, normed, preferred_element_type=jnp.float32)
    grad_normed = jnp.dot(grad_qkv, qkv_weight, preferred_element_type=jnp.float32)
    grad_gain = jnp.sum(grad_normed * unit, axis=0)
    scaled = grad_normed * gain_value
    grad_x = inverse * (
        scaled
        - jnp.mean(scaled, axis=-1, keepdims=True)
        - unit * jnp.mean(scaled * unit, axis=-1, keepdims=True)
    )
    grad_table = gather_bias(jnp.sum(grad_scores, axis=1), onehot)
    return (grad_x.reshape(groups, count, WT, C), grad_qkv_w, grad_proj, grad_gain, grad_table)


def body(tokens, grad_out, qkv_weight, proj_weight, norm_gain, bias_table):
    full_qkv, full_proj, full_gain = (
        lax.all_gather(qkv_weight, "dp", axis=0, tiled=True),
        lax.all_gather(proj_weight, "dp", axis=0, tiled=True),
        lax.all_gather(norm_gain, "dp", axis=0, tiled=True),
    )
    members, levels, lat_rows, lon_cols = (
        tokens.shape[0],
        tokens.shape[1],
        tokens.shape[2],
        tokens.shape[3],
    )
    ahead = passed_along((tokens[:, :, :, :SO], grad_out[:, :, :, :SO]), "lon", -1)
    lon_tokens = jnp.concatenate([tokens[:, :, :, SO:], ahead[0]], axis=3)
    lon_grads = jnp.concatenate([grad_out[:, :, :, SO:], ahead[1]], axis=3)
    above = passed_along((lon_tokens[:, :, :SA], lon_grads[:, :, :SA]), "lat", -1)
    shifted = jnp.concatenate([lon_tokens[:, :, SA:], above[0]], axis=2)
    shifted_dy = jnp.concatenate([lon_grads[:, :, SA:], above[1]], axis=2)
    pole_device = lax.axis_index("lat") == lax.axis_size("lat") - 1
    wrapped = jnp.logical_and(jnp.arange(lat_rows) >= lat_rows - SA, pole_device)
    grid_shape = (members, levels, lat_rows, lon_cols, 1)
    flag_grid = jnp.broadcast_to(wrapped[None, None, :, None, None], grid_shape)
    outputs = window_grads(
        to_windows(shifted, lat_rows, lon_cols),
        to_windows(shifted_dy, lat_rows, lon_cols),
        to_windows(flag_grid, lat_rows, lon_cols)[..., 0],
        bias_table,
        full_qkv,
        full_proj,
        full_gain,
        offsets_table(),
    )
    grad_blocks, grad_qkv_w, grad_proj, grad_gain, grad_table = outputs
    table_sum = lax.psum(grad_table, ("lon", "dp"))
    grad_shifted = from_windows(grad_blocks, members, lat_rows, lon_cols)
    below = passed_along(grad_shifted[:, :, lat_rows - SA :].astype(jnp.bfloat16), "lat", 1).astype(
        jnp.float32
    )
    lat_restored = jnp.concatenate([below, grad_shifted[:, :, : lat_rows - SA]], axis=2)
    behind = passed_along(shortened(lat_restored[:, :, :, lon_cols - SO :]), "lon", 1)
    restored = jnp.concatenate([behind, lat_restored[:, :, :, : lon_cols - SO]], axis=3)
    grad_tokens = (grad_out.astype(jnp.float32) + restored).astype(jnp.bfloat16)
    summed = lax.psum((grad_qkv_w, grad_proj, grad_gain), ("lon", "lat"))
    shares = (
        lax.psum_scatter(
            summed[0].astype(jnp.bfloat16), "dp", scatter_dimension=0, tiled=True
        ).astype(jnp.float32),
        lax.psum_scatter(
            summed[1].astype(jnp.bfloat16), "dp", scatter_dimension=0, tiled=True
        ).astype(jnp.float32),
        lax.psum_scatter(
            summed[2].astype(jnp.bfloat16), "dp", scatter_dimension=0, tiled=True
        ).astype(jnp.float32),
    )
    return (grad_tokens, shares[0], shares[1], shares[2], table_sum)


def solution(mesh):
    return jax.shard_map(
        body,
        mesh=mesh,
        in_specs=(
            P("dp", None, "lat", "lon", None),
            P("dp", None, "lat", "lon", None),
            P("dp", None),
            P("dp", None),
            P("dp"),
            P("lat", None, None),
        ),
        out_specs=(
            P("dp", None, "lat", "lon", None),
            P("dp", None),
            P("dp", None),
            P("dp"),
            P("lat", None, None),
        ),
        check_vma=False,
    )
```

profile of v0, /device:TPU:0, one launch (start us, length us, event | category | flops | bytes accessed | tf_op | source)
XLA Modules:
  0.0 192.5 jit_solution(13003009651287583203)
XLA Ops:
  8.1 0.9 fusion.26
  9.0 2.5 %collective-permute-start = (bf16[1,2,6,6,192]{4,1,3,2,0:T(2,128)(2,1)S(1)}, bf16[1,2,6,6,192]{4,1,3,2,0:T(2,128)(2,1)S(1)}, u32[]{:S(2)}, u32[]{:S(2)}) collective-permute-start(bf16[1,2,6,6,192]{4,1,3,2,0:T(2,128)(2,1)S(1)} %get-tuple-element.24), channel_id=1, source_target_pairs={{0,24},{8,0},{16,8},{24,16},{1,25},{9,1},{17,9},{25,17},{2,26},{10... | collective-permute-start | bytes 82952 | tf_op jit(solution)/shard_map/ppermute | solution.py:24
  13.0 1.1 reduce.8
  14.8 4.9 %convolution_bitcast_fusion = f32[1,6,12,12,12,12]{4,5,2,1,3,0:T(8,128)} fusion(f32[6,12,12,23,1]{3,2,1,0,4:T(8,128)S(1)} %reshape.415, pred[12,12,23,1,1]{2,0,1,4,3:T(8,128)(4,1)S(1)} %fusion.16), kind=kOutput, calls=%fused_computation.1 | convolution fusion | flops 34338816 | bytes 580464 | tf_op jit(solution)/shard_map/ghabr,uvr->ghaubv/dot_general | solution.py:41
  19.7 6.3 %all_gather.10 = bf16[576,192]{1,0:T(8,128)(2,1)S(1)} all-gather(bf16[288,192]{1,0:T(8,128)(2,1)S(1)} %copy-done.5), channel_id=1, replica_groups=mesh['lon'=4,'lat'=4,'dp'=2] {'dp'}, dimensions={0}, use_global_device_ids=true | all-gather | bytes 331776 | tf_op jit(solution)/shard_map/all_gather | solution.py:147
  27.4 4.9 %all-reduce = bf16[192]{0:T(256)(128)(2,1)S(1)} all-reduce(bf16[192]{0:T(256)(128)(2,1)S(1)} %dynamic-update-slice), channel_id=1, replica_groups=mesh['lon'=4,'lat'=4,'dp'=2] {'dp'}, use_global_device_ids=true, to_apply=%add | all-reduce | flops 192 | bytes 768
  32.4 11.7 %copy.70 = f32[1,6,12,12,12,12]{3,2,5,4,1,0:T(8,128)} copy(f32[1,6,12,12,12,12]{4,5,2,1,3,0:T(8,128)} %convolution_bitcast_fusion) | data formatting | bytes 995328 | tf_op jit(solution)/shard_map/broadcast_in_dim;reshape | solution.py:94
  44.1 4.9 %reshape.419 = f32[6,144,144]{1,2,0:T(8,128)S(1)} reshape(f32[1,6,12,12,12,12]{3,2,5,4,1,0:T(8,128)} %copy.70) | data formatting | bytes 995328 | tf_op jit(solution)/shard_map/broadcast_in_dim;reshape | solution.py:94
  49.0 4.8 %all_gather.11 = bf16[192,192]{1,0:T(8,128)(2,1)S(1)} all-gather(bf16[96,192]{1,0:T(8,128)(2,1)S(1)} %copy-done.9), channel_id=1, replica_groups=mesh['lon'=4,'lat'=4,'dp'=2] {'dp'}, dimensions={0}, use_global_device_ids=true | all-gather | bytes 110592 | tf_op jit(solution)/shard_map/all_gather | solution.py:148
  53.9 3.7 %collective-permute-start.1 = (bf16[1,2,3,12,192]{4,1,3,2,0:T(2,128)(2,1)S(1)}, bf16[1,2,3,12,192]{4,1,3,2,0:T(2,128)(2,1)S(1)}, u32[]{:S(2)}, u32[]{:S(2)}) collective-permute-start(bf16[1,2,3,12,192]{4,1,3,2,0:T(2,128)(2,1)S(1)} %get-tuple-element.22), channel_id=1, source_target_pairs={{0,6},{2,0},{4,2},{6,4},{1,7},{3,1},{5,3},{7,5},{8,14},{10,8},{12,... | collective-permute-start | bytes 82952 | tf_op jit(solution)/shard_map/ppermute | solution.py:24
  60.4 1.5 collective-permute-done.3
  64.6 1.9 convolution_bitcast_fusion.2
  66.5 1.2 multiply_reduce_fusion
  69.0 1.0 convolution_convert_fusion.1
  70.1 5.0 %reshape.406 = f32[6,12,12,12,12]{2,1,4,3,0:T(8,128)} reshape(f32[6,144,144]{1,2,0:T(8,128)S(1)} %subtract_multiply_fusion) | data formatting | bytes 995328 | tf_op jit(solution)/shard_map/reshape.46
  76.3 6.0 %convolution_bitcast_fusion.1 = f32[6,12,12,23]{3,1,2,0:T(8,128)S(1)} fusion(f32[6,12,12,12,12]{2,1,4,3,0:T(8,128)} %reshape.406, s32[12,12]{0,1:T(8,128)S(1)} %copy-done.8), kind=kOutput, calls=%fused_computation.7 | convolution fusion | flops 34342128 | bytes 577728 | tf_op jit(solution)/shard_map/ghaubv,uvr->ghabr/dot_general | solution.py:48
  82.5 0.9 reshape.407
  83.4 77.7 %all-reduce.7 = (bf16[576,192]{1,0:T(8,128)(2,1)}, bf16[192,192]{1,0:T(8,128)(2,1)}, bf16[192]{0:T(256)(128)(2,1)S(1)}) all-reduce(f32[576,192]{1,0:T(8,128)S(1)} %fusion.30, f32[192,192]{1,0:T(8,128)S(1)} %fusion.31, f32[192]{0:T(256)S(1)} %get-tuple-element.15), channel_id=1, replica_groups=mesh['lon'=4,'lat'=4,'dp'=2] {'lon','lat'}, use_global_device_ids=true, to_apply=%region_7.8 | all-reduce | flops 147648 | bytes 885888 | tf_op jit(solution)/shard_map/psum | solution.py:187
  162.2 4.9 %all-reduce.1 = bf16[192]{0:T(256)(128)(2,1)S(1)} all-reduce(bf16[192]{0:T(256)(128)(2,1)S(1)} %get-tuple-element.20), channel_id=4, replica_groups=mesh['lon'=4,'lat'=4,'dp'=2] {'dp'}, use_global_device_ids=true, to_apply=%region_13.14.clone | all-reduce | flops 192 | bytes 768
  168.1 1.6 copy.60
  169.7 1.3 collective-permute-done.5
  171.8 1.4 convert_element_type.150
  173.2 10.2 %reduce-scatter.3.cloned.1.call-done = bf16[288,192]{1,0:T(8,128)(2,1)} async-done(((bf16[576,192]{1,0:T(8,128)(2,1)}), bf16[288,192]{1,0:T(8,128)(2,1)}) %reduce-scatter.3.cloned.1.call-update) | async-done | bytes 110608 | tf_op jit(solution)/shard_map/reduce_scatter | solution.py:189
  183.4 1.6 convert_element_type.145
  (106 shorter events, 13.2 us)
Async XLA Ops:
  8.0 17.9 %copy-start.15 = (u32[32]{0:T(128)S(1)}, u32[32]{0:T(128)}, u32[]{:S(2)}) copy-start(u32[32]{0:T(128)} %constant.36) | copy-start | bytes 388
  8.0 11.7 %copy-start.5 = (bf16[288,192]{1,0:T(8,128)(2,1)S(1)}, bf16[288,192]{1,0:T(8,128)(2,1)}, u32[]{:S(2)}) copy-start(bf16[288,192]{1,0:T(8,128)(2,1)} %param.8) | copy-start | bytes 331780
  8.0 19.2 %copy-start.16 = (bf16[96]{0:T(256)(128)(2,1)S(1)}, bf16[96]{0:T(256)(128)(2,1)}, u32[]{:S(2)}) copy-start(bf16[96]{0:T(256)(128)(2,1)} %param.10) | copy-start | bytes 580
  8.0 160.1 %all-reduce.6.cloned.1.call-start = ((), (), s32[]{:S(2)}) async-start(), calls=%async_computation.4 | async-start | bytes 212992 | tf_op jit(solution)/shard_map/psum | solution.py:178
  9.0 44.9 %collective-permute-start = (bf16[1,2,6,6,192]{4,1,3,2,0:T(2,128)(2,1)S(1)}, bf16[1,2,6,6,192]{4,1,3,2,0:T(2,128)(2,1)S(1)}, u32[]{:S(2)}, u32[]{:S(2)}) collective-permute-start(bf16[1,2,6,6,192]{4,1,3,2,0:T(2,128)(2,1)S(1)} %get-tuple-element.24), channel_id=1, source_target_pairs={{0,24},{8,0},{16,8},{24,16},{1,25},{9,1},{17,9},{25,17},{2,26},{10... | collective-permute-start | bytes 82952 | tf_op jit(solution)/shard_map/ppermute | solution.py:24
  12.3 45.3 %collective-permute-start.2 = (bf16[1,2,6,6,192]{4,1,3,2,0:T(2,128)(2,1)S(1)}, bf16[1,2,6,6,192]{4,1,3,2,0:T(2,128)(2,1)S(1)}, u32[]{:S(2)}, u32[]{:S(2)}) collective-permute-start(bf16[1,2,6,6,192]{4,1,3,2,0:T(2,128)(2,1)S(1)} %get-tuple-element.28), channel_id=1, source_target_pairs={{0,24},{8,0},{16,8},{24,16},{1,25},{9,1},{17,9},{25,17},{2,26},{10... | collective-permute-start | bytes 82952 | tf_op jit(solution)/shard_map/ppermute | solution.py:24
  13.0 19.4 %copy-start.7 = (s32[12,12]{0,1:T(8,128)}, s32[12,12]{0,1:T(8,128)S(1)}, u32[]{:S(2)}) copy-start(s32[12,12]{0,1:T(8,128)S(1)} %subtract_add_fusion) | copy-start | bytes 1732
  44.1 5.0 %copy-start.9 = (bf16[96,192]{1,0:T(8,128)(2,1)S(1)}, bf16[96,192]{1,0:T(8,128)(2,1)}, u32[]{:S(2)}) copy-start(bf16[96,192]{1,0:T(8,128)(2,1)} %param.9) | copy-start | bytes 110596
  53.9 5.3 %collective-permute-start.1 = (bf16[1,2,3,12,192]{4,1,3,2,0:T(2,128)(2,1)S(1)}, bf16[1,2,3,12,192]{4,1,3,2,0:T(2,128)(2,1)S(1)}, u32[]{:S(2)}, u32[]{:S(2)}) collective-permute-start(bf16[1,2,3,12,192]{4,1,3,2,0:T(2,128)(2,1)S(1)} %get-tuple-element.22), channel_id=1, source_target_pairs={{0,6},{2,0},{4,2},{6,4},{1,7},{3,1},{5,3},{7,5},{8,14},{10,8},{12,... | collective-permute-start | bytes 82952 | tf_op jit(solution)/shard_map/ppermute | solution.py:24
  57.7 4.2 %collective-permute-start.3 = (bf16[1,2,3,12,192]{4,1,3,2,0:T(2,128)(2,1)S(1)}, bf16[1,2,3,12,192]{4,1,3,2,0:T(2,128)(2,1)S(1)}, u32[]{:S(2)}, u32[]{:S(2)}) collective-permute-start(bf16[1,2,3,12,192]{4,1,3,2,0:T(2,128)(2,1)S(1)} %get-tuple-element.26), channel_id=1, source_target_pairs={{0,6},{2,0},{4,2},{6,4},{1,7},{3,1},{5,3},{7,5},{8,14},{10,8},{12,... | collective-permute-start | bytes 82952 | tf_op jit(solution)/shard_map/ppermute | solution.py:24
  59.7 3.7 %copy-start.2 = (f32[2,6,12]{0,2,1:T(8,128)}, f32[2,6,12]{0,2,1:T(8,128)S(1)}, u32[]{:S(2)}) copy-start(f32[2,6,12]{0,2,1:T(8,128)S(1)} %add_rsqrt_fusion) | copy-start | bytes 1732
  60.1 3.3 %copy-start.11 = (f32[144]{0:T(256)}, f32[144]{0:T(256)S(1)}, u32[]{:S(2)}) copy-start(f32[144]{0:T(256)S(1)} %div.25) | copy-start | bytes 1732
  64.6 3.1 %copy-start.10 = (f32[6,144]{1,0:T(8,128)}, f32[6,144]{1,0:T(8,128)S(1)}, u32[]{:S(2)}) copy-start(f32[6,144]{1,0:T(8,128)S(1)} %get-tuple-element.31) | copy-start | bytes 10372
  68.5 6.5 %copy-start.6 = (bf16[1,1,144,1,6,32]{2,5,4,3,1,0:T(8,128)(2,1)S(1)}, bf16[1,1,144,1,6,32]{2,5,4,3,1,0:T(8,128)(2,1)}, u32[]{:S(2)}) copy-start(bf16[1,1,144,1,6,32]{2,5,4,3,1,0:T(8,128)(2,1)} %convolution_bitcast_fusion.2) | copy-start | bytes 165892
  68.5 6.6 %copy-start.12 = (f32[144]{0:T(256)S(1)}, f32[144]{0:T(256)}, u32[]{:S(2)}) copy-start(f32[144]{0:T(256)} %copy-done.11) | copy-start | bytes 1732
  68.5 6.6 %copy-start.14 = (f32[144]{0:T(256)S(1)}, f32[144]{0:T(256)}, u32[]{:S(2)}) copy-start(f32[144]{0:T(256)} %copy-done.13) | copy-start | bytes 1732
  68.8 6.8 %copy-start.1 = (bf16[1,2,3,12,192]{4,1,3,2,0:T(2,128)(2,1)S(1)}, bf16[1,2,3,12,192]{4,1,3,2,0:T(2,128)(2,1)}, u32[]{:S(2)}) copy-start(bf16[1,2,3,12,192]{4,1,3,2,0:T(2,128)(2,1)} %copy-done) | copy-start | bytes 82948
  68.8 6.7 %copy-start.3 = (f32[2,6,12]{0,2,1:T(8,128)S(1)}, f32[2,6,12]{0,2,1:T(8,128)}, u32[]{:S(2)}) copy-start(f32[2,6,12]{0,2,1:T(8,128)} %copy-done.2) | copy-start | bytes 1732
  69.0 7.3 %copy-start.8 = (s32[12,12]{0,1:T(8,128)S(1)}, s32[12,12]{0,1:T(8,128)}, u32[]{:S(2)}) copy-start(s32[12,12]{0,1:T(8,128)} %copy-done.7) | copy-start | bytes 1732
  75.8 95.2 %copy-start.4 = (bf16[1,2,6,12,192]{4,1,3,2,0:T(2,128)(2,1)S(1)}, bf16[1,2,6,12,192]{4,1,3,2,0:T(2,128)(2,1)}, u32[]{:S(2)}) copy-start(bf16[1,2,6,12,192]{4,1,3,2,0:T(2,128)(2,1)} %param.7) | copy-start | bytes 165892
  83.4 88.4 %reduce-scatter.5.cloned.1.call-start = ((), (), s32[]{:S(2)}) async-start(), calls=%async_computation.3 | async-start | bytes 147456 | tf_op jit(solution)/shard_map/reduce_scatter | solution.py:192
  161.2 22.2 %reduce-scatter.3.cloned.1.call-start = ((), (), s32[]{:S(2)}) async-start(), calls=%async_computation.2 | async-start | bytes 442368 | tf_op jit(solution)/shard_map/reduce_scatter | solution.py:189
  161.5 5.9 %collective-permute-start.4 = (bf16[1,2,3,12,192]{4,3,2,1,0:T(8,128)(2,1)S(1)}, bf16[1,2,3,12,192]{4,3,2,1,0:T(8,128)(2,1)S(1)}, u32[]{:S(2)}, u32[]{:S(2)}) collective-permute-start(bf16[1,2,3,12,192]{4,3,2,1,0:T(8,128)(2,1)S(1)} %slice.103), channel_id=1, source_target_pairs={{0,2},{2,4},{4,6},{6,0},{1,3},{3,5},{5,7},{7,1},{8,10},{10,12},{12... | collective-permute-start | bytes 82952 | tf_op jit(solution)/shard_map/ppermute | solution.py:24
  167.4 3.6 %collective-permute-start.5 = (bf16[1,2,6,6,192]{4,3,2,1,0:T(8,128)(2,1)S(1)}, bf16[1,2,6,6,192]{4,3,2,1,0:T(8,128)(2,1)S(1)}, u32[]{:S(2)}, u32[]{:S(2)}) collective-permute-start(bf16[1,2,6,6,192]{4,3,2,1,0:T(8,128)(2,1)S(1)} %fusion.15), channel_id=1, source_target_pairs={{0,8},{8,16},{16,24},{24,0},{1,9},{9,17},{17,25},{25,1},{2,10},{10... | collective-permute-start | bytes 82952 | tf_op jit(solution)/shard_map/ppermute | solution.py:24
  (2 other events, 3.7 us)
Sparse Core Ops, SparseCore 0:
  83.5 51.0 all-reduce.5
Sparse Core Ops, SparseCore 1:
  161.3 7.5 reduce-scatter.4
  171.5 11.9 reduce-scatter.2
where the time goes:
time: 193 us
  blocking collectives  98.6 us (51%)
  local copies, waits for them, and re-layouts  29.6 us (15%)
  between operations  17.3 us (9%)
  matrix products  17 us (9%)
  waiting for transfers between devices  14.2 us (7%)
  other arithmetic  8 us (4%)
  starting transfers between devices  7.77 us (4%)
    psum x1, blocking collectives, body(): summed = lax.psum((grad_qkv_w, grad_proj, grad_gain), ('lon', 'lat'))  77.7 us
    another operation x2, local copies, waits for them, and re-layouts, window_grads(): scores = scores + bias_full[:, None]  16.6 us
    reduce_scatter x1, waiting for transfers between devices, body(): lax.psum_scatter(summed[0].astype(jnp.bfloat16), 'dp', scatter_dimension=...  10.2 us
    unnamed x2, blocking collectives  9.86 us
    ppermute x6, starting transfers between devices, passed_along(): return lax.ppermute(value, axis, pairs)  7.64 us
    all_gather x1, blocking collectives, body(): lax.all_gather(qkv_weight, 'dp', axis=0, tiled=True)  6.26 us
    dot_general x1, matrix products, gather_bias(): jnp.einsum('ghaubv,uvr->ghabr', shaped, onehot, precision=lax.Precision.H...  5.99 us
    another operation x2, local copies, waits for them, and re-layouts  5.3 us
  transfers between devices with their start and end apart: 9, of which 5 were waited for; matrix products, arithmetic and copies ran while one was open for 16% of the time, Pallas kernels for 0%

commit v1 on v0

--- a/solution.py
+++ b/solution.py
@@ -184,7 +184,7 @@
     behind = passed_along(shortened(lat_restored[:, :, :, lon_cols - SO :]), "lon", 1)
     restored = jnp.concatenate([behind, lat_restored[:, :, :, : lon_cols - SO]], axis=3)
     grad_tokens = (grad_out.astype(jnp.float32) + restored).astype(jnp.bfloat16)
-    summed = lax.psum((grad_qkv_w, grad_proj, grad_gain), ("lon", "lat"))
+    summed = lax.psum(lax.psum((grad_qkv_w, grad_proj, grad_gain), "lat"), "lon")
     shares = (
         lax.psum_scatter(
             summed[0].astype(jnp.bfloat16), "dp", scatter_dimension=0, tiled=True

time: 193 us -> 221 us (1.15)
  waiting for transfers between devices: 14.2 us -> 86.1 us
  blocking collectives: 98.6 us -> 53.6 us
    psum x1 -> x2, blocking collectives: 77.7 us -> 32.5 us  [the longest x1 21.4 us: body(): lax.psum(lax.psum((grad_qkv_w, grad_proj, grad_gain), 'lat'), 'lon')]
    psum x0 -> x1, waiting for transfers between devices: none -> 34 us  [body(): lax.psum((grad_qkv_w, grad_proj, grad_gain), 'lat')]
    psum x1, waiting for transfers between devices: 0.01 us -> 25.6 us  [body(): table_sum = lax.psum(grad_table, ('lon', 'dp'))]
    reduce_scatter x1, waiting for transfers between devices: 0.01 us -> 5.61 us  [body(): lax.psum_scatter(summed[1].astype(jnp.bfloat16), 'dp', scatter_dimension=...]
    ppermute x6, waiting for transfers between devices: 3.91 us -> 7.45 us  [passed_along(): return lax.ppermute(value, axis, pairs)]
    reduce_scatter x1, waiting for transfers between devices: 10.2 us -> 13.4 us  [body(): lax.psum_scatter(summed[0].astype(jnp.bfloat16), 'dp', scatter_dimension=...]
  transfers between devices with their start and end apart: 9 -> 10, of which waited for: 5 -> 7; matrix products, arithmetic and copies ran while one was open for 16% -> 17% of each run, Pallas kernels for 0% -> 0%
where the time goes in v1:
time: 221 us; the launch traced here: 220 us
  waiting for transfers between devices  86.1 us (39%)
  blocking collectives  53.6 us (24%)
  local copies, waits for them, and re-layouts  29.6 us (13%)
  matrix products  18.6 us (8%)
  between operations  15.6 us (7%)
  starting transfers between devices  8.61 us (4%)
  other arithmetic  8 us (4%)
    psum x1, waiting for transfers between devices, body(): lax.psum((grad_qkv_w, grad_proj, grad_gain), 'lat')  34 us
    psum x1, waiting for transfers between devices, body(): table_sum = lax.psum(grad_table, ('lon', 'dp'))  25.6 us
    psum x1, blocking collectives, body(): lax.psum(lax.psum((grad_qkv_w, grad_proj, grad_gain), 'lat'), 'lon')  21.4 us
    another operation x2, local copies, waits for them, and re-layouts, window_grads(): scores = scores + bias_full[:, None]  16.6 us
    reduce_scatter x1, waiting for transfers between devices, body(): lax.psum_scatter(summed[0].astype(jnp.bfloat16), 'dp', scatter_dimension=...  13.4 us
    psum x1, blocking collectives, body(): lax.psum((grad_qkv_w, grad_proj, grad_gain), 'lat')  11.1 us
    unnamed x2, blocking collectives  10 us
    ppermute x6, starting transfers between devices, passed_along(): return lax.ppermute(value, axis, pairs)  8.26 us
  transfers between devices with their start and end apart: 10, of which 7 were waited for; matrix products, arithmetic and copies ran while one was open for 17% of the time, Pallas kernels for 0%

profile of v1, /device:TPU:0, one launch (start us, length us, event | category | flops | bytes accessed | tf_op | source)
XLA Modules:
  0.0 220.1 jit_solution(9611155773095604916)
XLA Ops:
  8.1 2.5 %collective-permute-start = (bf16[1,2,6,6,192]{4,1,3,2,0:T(2,128)(2,1)S(1)}, bf16[1,2,6,6,192]{4,1,3,2,0:T(2,128)(2,1)S(1)}, u32[]{:S(2)}, u32[]{:S(2)}) collective-permute-start(bf16[1,2,6,6,192]{4,1,3,2,0:T(2,128)(2,1)S(1)} %get-tuple-element.26), channel_id=1, source_target_pairs={{0,24},{8,0},{16,8},{24,16},{1,25},{9,1},{17,9},{25,17},{2,26},{10... | collective-permute-start | bytes 82952 | tf_op jit(solution)/shard_map/ppermute | solution.py:24
  14.0 4.9 %convolution_bitcast_fusion = f32[1,6,12,12,12,12]{4,5,2,1,3,0:T(8,128)} fusion(f32[6,12,12,23,1]{3,2,1,0,4:T(8,128)S(1)} %reshape.415, pred[12,12,23,1,1]{2,0,1,4,3:T(8,128)(4,1)S(1)} %fusion.16), kind=kOutput, calls=%fused_computation.1 | convolution fusion | flops 34338816 | bytes 580464 | tf_op jit(solution)/shard_map/ghabr,uvr->ghaubv/dot_general | solution.py:41
  18.9 6.3 %all_gather.10 = bf16[576,192]{1,0:T(8,128)(2,1)S(1)} all-gather(bf16[288,192]{1,0:T(8,128)(2,1)S(1)} %copy-done.5), channel_id=1, replica_groups=mesh['lon'=4,'lat'=4,'dp'=2] {'dp'}, dimensions={0}, use_global_device_ids=true | all-gather | bytes 331776 | tf_op jit(solution)/shard_map/all_gather | solution.py:147
  26.6 4.9 %all-reduce = bf16[192]{0:T(256)(128)(2,1)S(1)} all-reduce(bf16[192]{0:T(256)(128)(2,1)S(1)} %dynamic-update-slice), channel_id=1, replica_groups=mesh['lon'=4,'lat'=4,'dp'=2] {'dp'}, use_global_device_ids=true, to_apply=%add | all-reduce | flops 192 | bytes 768
  31.5 11.7 %copy.70 = f32[1,6,12,12,12,12]{3,2,5,4,1,0:T(8,128)} copy(f32[1,6,12,12,12,12]{4,5,2,1,3,0:T(8,128)} %convolution_bitcast_fusion) | data formatting | bytes 995328 | tf_op jit(solution)/shard_map/broadcast_in_dim;reshape | solution.py:94
  43.3 4.9 %reshape.419 = f32[6,144,144]{1,2,0:T(8,128)S(1)} reshape(f32[1,6,12,12,12,12]{3,2,5,4,1,0:T(8,128)} %copy.70) | data formatting | bytes 995328 | tf_op jit(solution)/shard_map/broadcast_in_dim;reshape | solution.py:94
  48.2 4.8 %all_gather.11 = bf16[192,192]{1,0:T(8,128)(2,1)S(1)} all-gather(bf16[96,192]{1,0:T(8,128)(2,1)S(1)} %copy-done.9), channel_id=1, replica_groups=mesh['lon'=4,'lat'=4,'dp'=2] {'dp'}, dimensions={0}, use_global_device_ids=true | all-gather | bytes 110592 | tf_op jit(solution)/shard_map/all_gather | solution.py:148
  53.1 3.7 %collective-permute-start.1 = (bf16[1,2,3,12,192]{4,1,3,2,0:T(2,128)(2,1)S(1)}, bf16[1,2,3,12,192]{4,1,3,2,0:T(2,128)(2,1)S(1)}, u32[]{:S(2)}, u32[]{:S(2)}) collective-permute-start(bf16[1,2,3,12,192]{4,1,3,2,0:T(2,128)(2,1)S(1)} %get-tuple-element.24), channel_id=1, source_target_pairs={{0,6},{2,0},{4,2},{6,4},{1,7},{3,1},{5,3},{7,5},{8,14},{10,8},{12,... | collective-permute-start | bytes 82952 | tf_op jit(solution)/shard_map/ppermute | solution.py:24
  59.5 1.4 collective-permute-done.3
  63.6 1.9 convolution_bitcast_fusion.2
  65.4 1.2 multiply_reduce_fusion
  69.0 5.0 %reshape.406 = f32[6,12,12,12,12]{2,1,4,3,0:T(8,128)} reshape(f32[6,144,144]{1,2,0:T(8,128)S(1)} %subtract_multiply_fusion) | data formatting | bytes 995328 | tf_op jit(solution)/shard_map/reshape.46
  76.8 11.1 %psum.53 = f32[192]{0:T(256)S(1)} all-reduce(f32[192]{0:T(256)S(1)} %get-tuple-element.15), channel_id=1, replica_groups=mesh['lon'=4,'lat'=4,'dp'=2] {'lat'}, use_global_device_ids=true, to_apply=%region_14.15 | all-reduce | flops 192 | bytes 1536 | tf_op jit(solution)/shard_map/psum | solution.py:187
  88.2 6.1 %convolution_bitcast_fusion.1 = f32[6,12,12,23]{3,1,2,0:T(8,128)S(1)} fusion(f32[6,12,12,12,12]{2,1,4,3,0:T(8,128)} %reshape.406, s32[12,12]{0,1:T(8,128)S(1)} %copy-done.8), kind=kOutput, calls=%fused_computation.7 | convolution fusion | flops 34342128 | bytes 577728 | tf_op jit(solution)/shard_map/ghaubv,uvr->ghabr/dot_general | solution.py:48
  95.4 34.0 %all-reduce.10.cloned.1.call-done = (f32[576,192]{1,0:T(8,128)}, f32[192,192]{1,0:T(8,128)}) async-done(((f32[576,192]{1,0:T(8,128)}, f32[192,192]{1,0:T(8,128)}), (f32[576,192]{1,0:T(8,128)}, f32[192,192]{1,0:T(8,128)})) %all-reduce.10.cloned.1.call-update) | async-done | bytes 589840 | tf_op jit(solution)/shard_map/psum | solution.py:187
  129.4 21.4 %all-reduce.11 = (bf16[576,192]{1,0:T(8,128)(2,1)}, bf16[192,192]{1,0:T(8,128)(2,1)}, bf16[192]{0:T(256)(128)(2,1)S(1)}) all-reduce(f32[576,192]{1,0:T(8,128)} %get-tuple-element.18, f32[192,192]{1,0:T(8,128)} %get-tuple-element.19, f32[192]{0:T(256)S(1)} %psum.53), channel_id=1, replica_groups=mesh['lon'=4,'lat'=4,'dp'=2] {'lon'}, use_global_device_ids=true, to_apply=%region_8.9 | all-reduce | flops 147648 | bytes 885888 | tf_op jit(solution)/shard_map/psum | solution.py:187
  152.0 5.1 %collective-permute-done.4 = bf16[1,2,3,12,192]{4,3,2,1,0:T(8,128)(2,1)S(1)} collective-permute-done((bf16[1,2,3,12,192]{4,3,2,1,0:T(8,128)(2,1)S(1)}, bf16[1,2,3,12,192]{4,3,2,1,0:T(8,128)(2,1)S(1)}, u32[]{:S(2)}, u32[]{:S(2)}) %collective-permute-start.4) | collective-permute-done | bytes 27680 | tf_op jit(solution)/shard_map/ppermute | solution.py:24
  157.8 25.6 %all-reduce.8.cloned.1.call-done = f32[1,6,3312]{2,1,0:T(8,128)} async-done(((f32[1,6,3312]{2,1,0:T(8,128)}), f32[1,6,3312]{2,1,0:T(8,128)}) %all-reduce.8.cloned.1.call-update) | async-done | bytes 79504 | tf_op jit(solution)/shard_map/psum | solution.py:178
  183.4 1.6 copy.60
  185.8 5.1 %all-reduce.1 = bf16[192]{0:T(256)(128)(2,1)S(1)} all-reduce(bf16[192]{0:T(256)(128)(2,1)S(1)} %get-tuple-element.22), channel_id=4, replica_groups=mesh['lon'=4,'lat'=4,'dp'=2] {'dp'}, use_global_device_ids=true, to_apply=%region_16.17.clone | all-reduce | flops 192 | bytes 768
  191.5 5.6 %reduce-scatter.5.cloned.1.call-done = bf16[96,192]{1,0:T(8,128)(2,1)} async-done(((bf16[192,192]{1,0:T(8,128)(2,1)}), bf16[96,192]{1,0:T(8,128)(2,1)}) %reduce-scatter.5.cloned.1.call-update) | async-done | bytes 36880 | tf_op jit(solution)/shard_map/reduce_scatter | solution.py:192
  197.1 1.4 convert_element_type.150
  198.6 13.4 %reduce-scatter.3.cloned.1.call-done = bf16[288,192]{1,0:T(8,128)(2,1)} async-done(((bf16[576,192]{1,0:T(8,128)(2,1)}), bf16[288,192]{1,0:T(8,128)(2,1)}) %reduce-scatter.3.cloned.1.call-update) | async-done | bytes 110608 | tf_op jit(solution)/shard_map/reduce_scatter | solution.py:189
  211.9 1.6 convert_element_type.145
  (110 shorter events, 19.4 us)
Async XLA Ops:
  7.2 17.9 %copy-start.15 = (u32[32]{0:T(128)S(1)}, u32[32]{0:T(128)}, u32[]{:S(2)}) copy-start(u32[32]{0:T(128)} %constant.36) | copy-start | bytes 388
  7.2 11.7 %copy-start.5 = (bf16[288,192]{1,0:T(8,128)(2,1)S(1)}, bf16[288,192]{1,0:T(8,128)(2,1)}, u32[]{:S(2)}) copy-start(bf16[288,192]{1,0:T(8,128)(2,1)} %param.8) | copy-start | bytes 331780
  7.2 19.2 %copy-start.16 = (bf16[96]{0:T(256)(128)(2,1)S(1)}, bf16[96]{0:T(256)(128)(2,1)}, u32[]{:S(2)}) copy-start(bf16[96]{0:T(256)(128)(2,1)} %param.10) | copy-start | bytes 580
  7.2 122.2 %all-reduce.10.cloned.1.call-start = ((), (), s32[]{:S(2)}) async-start(), calls=%async_computation.5 | async-start | bytes 1572864 | tf_op jit(solution)/shard_map/psum | solution.py:187
  8.1 44.9 %collective-permute-start = (bf16[1,2,6,6,192]{4,1,3,2,0:T(2,128)(2,1)S(1)}, bf16[1,2,6,6,192]{4,1,3,2,0:T(2,128)(2,1)S(1)}, u32[]{:S(2)}, u32[]{:S(2)}) collective-permute-start(bf16[1,2,6,6,192]{4,1,3,2,0:T(2,128)(2,1)S(1)} %get-tuple-element.26), channel_id=1, source_target_pairs={{0,24},{8,0},{16,8},{24,16},{1,25},{9,1},{17,9},{25,17},{2,26},{10... | collective-permute-start | bytes 82952 | tf_op jit(solution)/shard_map/ppermute | solution.py:24
  11.4 45.3 %collective-permute-start.2 = (bf16[1,2,6,6,192]{4,1,3,2,0:T(2,128)(2,1)S(1)}, bf16[1,2,6,6,192]{4,1,3,2,0:T(2,128)(2,1)S(1)}, u32[]{:S(2)}, u32[]{:S(2)}) collective-permute-start(bf16[1,2,6,6,192]{4,1,3,2,0:T(2,128)(2,1)S(1)} %get-tuple-element.30), channel_id=1, source_target_pairs={{0,24},{8,0},{16,8},{24,16},{1,25},{9,1},{17,9},{25,17},{2,26},{10... | collective-permute-start | bytes 82952 | tf_op jit(solution)/shard_map/ppermute | solution.py:24
  12.2 19.4 %copy-start.7 = (s32[12,12]{0,1:T(8,128)}, s32[12,12]{0,1:T(8,128)S(1)}, u32[]{:S(2)}) copy-start(s32[12,12]{0,1:T(8,128)S(1)} %subtract_add_fusion) | copy-start | bytes 1732
  43.2 5.0 %copy-start.9 = (bf16[96,192]{1,0:T(8,128)(2,1)S(1)}, bf16[96,192]{1,0:T(8,128)(2,1)}, u32[]{:S(2)}) copy-start(bf16[96,192]{1,0:T(8,128)(2,1)} %param.9) | copy-start | bytes 110596
  53.1 5.3 %collective-permute-start.1 = (bf16[1,2,3,12,192]{4,1,3,2,0:T(2,128)(2,1)S(1)}, bf16[1,2,3,12,192]{4,1,3,2,0:T(2,128)(2,1)S(1)}, u32[]{:S(2)}, u32[]{:S(2)}) collective-permute-start(bf16[1,2,3,12,192]{4,1,3,2,0:T(2,128)(2,1)S(1)} %get-tuple-element.24), channel_id=1, source_target_pairs={{0,6},{2,0},{4,2},{6,4},{1,7},{3,1},{5,3},{7,5},{8,14},{10,8},{12,... | collective-permute-start | bytes 82952 | tf_op jit(solution)/shard_map/ppermute | solution.py:24
  56.9 4.0 %collective-permute-start.3 = (bf16[1,2,3,12,192]{4,1,3,2,0:T(2,128)(2,1)S(1)}, bf16[1,2,3,12,192]{4,1,3,2,0:T(2,128)(2,1)S(1)}, u32[]{:S(2)}, u32[]{:S(2)}) collective-permute-start(bf16[1,2,3,12,192]{4,1,3,2,0:T(2,128)(2,1)S(1)} %get-tuple-element.28), channel_id=1, source_target_pairs={{0,6},{2,0},{4,2},{6,4},{1,7},{3,1},{5,3},{7,5},{8,14},{10,8},{12,... | collective-permute-start | bytes 82952 | tf_op jit(solution)/shard_map/ppermute | solution.py:24
  58.9 3.5 %copy-start.2 = (f32[2,6,12]{0,2,1:T(8,128)}, f32[2,6,12]{0,2,1:T(8,128)S(1)}, u32[]{:S(2)}) copy-start(f32[2,6,12]{0,2,1:T(8,128)S(1)} %add_rsqrt_fusion) | copy-start | bytes 1732
  59.3 3.1 %copy-start.11 = (f32[144]{0:T(256)}, f32[144]{0:T(256)S(1)}, u32[]{:S(2)}) copy-start(f32[144]{0:T(256)S(1)} %div.25) | copy-start | bytes 1732
  67.5 6.5 %copy-start.6 = (bf16[1,1,144,1,6,32]{2,5,4,3,1,0:T(8,128)(2,1)S(1)}, bf16[1,1,144,1,6,32]{2,5,4,3,1,0:T(8,128)(2,1)}, u32[]{:S(2)}) copy-start(bf16[1,1,144,1,6,32]{2,5,4,3,1,0:T(8,128)(2,1)} %convolution_bitcast_fusion.2) | copy-start | bytes 165892
  67.5 6.6 %copy-start.12 = (f32[144]{0:T(256)S(1)}, f32[144]{0:T(256)}, u32[]{:S(2)}) copy-start(f32[144]{0:T(256)} %copy-done.11) | copy-start | bytes 1732
  67.5 6.6 %copy-start.14 = (f32[144]{0:T(256)S(1)}, f32[144]{0:T(256)}, u32[]{:S(2)}) copy-start(f32[144]{0:T(256)} %copy-done.13) | copy-start | bytes 1732
  67.8 6.8 %copy-start.1 = (bf16[1,2,3,12,192]{4,1,3,2,0:T(2,128)(2,1)S(1)}, bf16[1,2,3,12,192]{4,1,3,2,0:T(2,128)(2,1)}, u32[]{:S(2)}) copy-start(bf16[1,2,3,12,192]{4,1,3,2,0:T(2,128)(2,1)} %copy-done) | copy-start | bytes 82948
  67.8 6.7 %copy-start.3 = (f32[2,6,12]{0,2,1:T(8,128)S(1)}, f32[2,6,12]{0,2,1:T(8,128)}, u32[]{:S(2)}) copy-start(f32[2,6,12]{0,2,1:T(8,128)} %copy-done.2) | copy-start | bytes 1732
  68.0 20.2 %copy-start.8 = (s32[12,12]{0,1:T(8,128)S(1)}, s32[12,12]{0,1:T(8,128)}, u32[]{:S(2)}) copy-start(s32[12,12]{0,1:T(8,128)} %copy-done.7) | copy-start | bytes 1732
  75.9 109.2 %copy-start.4 = (bf16[1,2,6,12,192]{4,1,3,2,0:T(2,128)(2,1)S(1)}, bf16[1,2,6,12,192]{4,1,3,2,0:T(2,128)(2,1)}, u32[]{:S(2)}) copy-start(bf16[1,2,6,12,192]{4,1,3,2,0:T(2,128)(2,1)} %param.7) | copy-start | bytes 165892
  87.9 95.5 %all-reduce.8.cloned.1.call-start = ((), (), s32[]{:S(2)}) async-start(), calls=%async_computation.4 | async-start | bytes 212992 | tf_op jit(solution)/shard_map/psum | solution.py:178
  95.3 101.8 %reduce-scatter.5.cloned.1.call-start = ((), (), s32[]{:S(2)}) async-start(), calls=%async_computation.3 | async-start | bytes 147456 | tf_op jit(solution)/shard_map/reduce_scatter | solution.py:192
  150.9 61.1 %reduce-scatter.3.cloned.1.call-start = ((), (), s32[]{:S(2)}) async-start(), calls=%async_computation.2 | async-start | bytes 442368 | tf_op jit(solution)/shard_map/reduce_scatter | solution.py:189
  151.1 5.9 %collective-permute-start.4 = (bf16[1,2,3,12,192]{4,3,2,1,0:T(8,128)(2,1)S(1)}, bf16[1,2,3,12,192]{4,3,2,1,0:T(8,128)(2,1)S(1)}, u32[]{:S(2)}, u32[]{:S(2)}) collective-permute-start(bf16[1,2,3,12,192]{4,3,2,1,0:T(8,128)(2,1)S(1)} %slice.103), channel_id=1, source_target_pairs={{0,2},{2,4},{4,6},{6,0},{1,3},{3,5},{5,7},{7,1},{8,10},{10,12},{12... | collective-permute-start | bytes 82952 | tf_op jit(solution)/shard_map/ppermute | solution.py:24
  157.1 27.9 %collective-permute-start.5 = (bf16[1,2,6,6,192]{4,3,2,1,0:T(8,128)(2,1)S(1)}, bf16[1,2,6,6,192]{4,3,2,1,0:T(8,128)(2,1)S(1)}, u32[]{:S(2)}, u32[]{:S(2)}) collective-permute-start(bf16[1,2,6,6,192]{4,3,2,1,0:T(8,128)(2,1)S(1)} %fusion.15), channel_id=1, source_target_pairs={{0,8},{8,16},{16,24},{24,0},{1,9},{9,17},{17,25},{25,1},{2,10},{10... | collective-permute-start | bytes 82952 | tf_op jit(solution)/shard_map/ppermute | solution.py:24
  (3 other events, 6.6 us)
Sparse Core Ops, SparseCore 0:
  88.0 41.3 all-reduce.9
  132.5 50.9 all-reduce.7
  186.3 10.7 reduce-scatter.4
  199.9 12.0 reduce-scatter.2
